TPU v7x, 128 devices: a whole 4x4x4 slice. The times are simulated.
128 devices in a mesh: dp: 32 (over x, y_lo, z), gz: 4 (over y_hi, core).
Axes of the slice: x: 4, y: 4 (y_hi: 2, y_lo: 2; y = y_hi * 2 + y_lo), z: 4, core: 2. Of those that a mesh axis runs over, the one named last changes fastest.
Arguments:
- field: bfloat16 [32, 16, 96, 9216], P('dp', None, 'gz'), may hold values from -6 to 6
- cotangent: bfloat16 [32, 16, 96, 9216], P('dp', None, 'gz'), may hold values from -36 to 36, as said below
- spec_weight: float32 [16, 16, 16, 256], P('gz'), may hold values from -1.5 to 1.5
- point_weight: bfloat16 [16, 16], replicated, may hold values from -1.5 to 1.5
- bias: float32 [16], replicated, may hold values from -3 to 3
Outputs:
- field_grad: bfloat16 [32, 16, 96, 9216], P('dp', None, 'gz')
- spectral_grad: float32 [16, 16, 16, 256], P('gz')
- point_grad: float32 [16, 16], replicated
- bias_grad: float32 [16], replicated
Inputs may be any that keep to these rules, and one draw needn't show every extreme that they name: `cotangent`: the gradient of the loss with respect to the layer's output.
All inputs are finite; a program needn't handle non-finite values.
Results may differ from a plain program's by a relative error of at most 0.007.
Values sent between devices are 32-bit elements; how exact they have to be, the bound alone decides.
No kernel may reach another device: no remote copies, remote signals or barrier semaphores. Data moves between devices by JAX's collectives and lax.ppermute only.
A program may use at most 192 MiB of HBM per device.

v0:
```python
import math
import jax
import jax.numpy as jnp
from jax import lax
from jax.sharding import PartitionSpec as P

N = 96
M = 16
root_half = 0.7071067811865476
density_norm = 0.3989422804014327


def basis_table(count_modes, length):
    mode_index = jnp.arange(count_modes, dtype=jnp.int32)
    half_count = count_modes // 2
    frequency = jnp.where(mode_index < half_count, mode_index, mode_index - half_count + 1)
    position = jnp.arange(length, dtype=jnp.int32)
    turns = frequency[:, None] * position[None, :] % length
    angle = turns.astype(jnp.float32) * (2.0 * math.pi / length)
    return jnp.where((mode_index < half_count)[:, None], jnp.cos(angle), jnp.sin(angle))


def kron_table(basis):
    outer = basis[:, None, :, None] * basis[None, :, None, :]
    return outer.reshape(M * M, N * N)


def gelu_slope(values):
    cumulative = 0.5 * (1.0 + lax.erf(values * root_half))
    return cumulative + values * jnp.exp(-0.5 * values * values) * density_norm


def shards(field, cotangent, spec_weight, point_weight, bias):
    highest = lax.Precision.HIGHEST
    samples_dev, channels, slab_rows, plane_cells = field.shape
    scale_fwd = (2.0 / N) ** 1.5
    scale_inv = (2.0 / M) ** 1.5
    basis = basis_table(M, N)
    kron = kron_table(basis)
    row_basis = lax.dynamic_slice_in_dim(basis, lax.axis_index("gz") * slab_rows, slab_rows, 1)
    contract_cells = (((1,), (1,)), ((), ()))

    def to_modes(values):
        flattened = values.reshape(samples_dev * channels * slab_rows, plane_cells).astype(
            jnp.float32
        )
        return lax.dot_general(flattened, kron, contract_cells, precision=highest).reshape(
            samples_dev, channels, slab_rows, M * M
        )

    def add_inverse(piece):
        piece_rows = piece.shape[0]
        inner = jnp.dot(
            piece.reshape(piece_rows * samples_dev * channels, M * M), kron, precision=highest
        )
        inner = inner.reshape(piece_rows, samples_dev, channels, plane_cells)
        return jnp.einsum("ax,asoz->soxz", row_basis, inner, precision=highest)

    line_modes = to_modes(field)
    rows_part = row_basis
    coefficients = lax.psum_scatter(
        scale_fwd * jnp.einsum("ax,scxp->ascp", rows_part, line_modes, precision=highest),
        "gz",
        scatter_dimension=0,
        tiled=True,
    )
    mixed_modes = jnp.einsum("asip,aiop->asop", coefficients, spec_weight, precision=highest)
    spectral = scale_inv * add_inverse(lax.all_gather(mixed_modes, "gz", axis=0, tiled=True))
    pre_act = (
        spectral
        + jnp.einsum("sixz,io->soxz", field, point_weight, preferred_element_type=jnp.float32)
        + bias[None, :, None, None]
    )
    grad_pre = (cotangent.astype(jnp.float32) * gelu_slope(pre_act)).astype(jnp.bfloat16)
    grad_line = to_modes(grad_pre)
    rows_part = row_basis
    grad_modes = lax.psum_scatter(
        scale_inv * jnp.einsum("ax,soxp->asop", rows_part, grad_line, precision=highest),
        "gz",
        scatter_dimension=0,
        tiled=True,
    )
    back_modes = jnp.einsum("aiop,asop->asip", spec_weight, grad_modes, precision=highest)
    field_spec = scale_fwd * add_inverse(lax.all_gather(back_modes, "gz", axis=0, tiled=True))
    field_grad = (
        field_spec
        + jnp.einsum("soxz,io->sixz", grad_pre, point_weight, preferred_element_type=jnp.float32)
    ).astype(jnp.bfloat16)
    local_point = jnp.einsum("sixz,soxz->io", field, grad_pre, preferred_element_type=jnp.float32)
    local_bias = jnp.sum(grad_pre, axis=(0, 2, 3), dtype=jnp.float32)
    total_point, total_bias = lax.psum((local_point, local_bias), ("dp", "gz"))
    local_spec = jnp.einsum("asip,asop->aiop", coefficients, grad_modes, precision=highest)
    grad_spec = lax.psum(local_spec, "dp")
    all_samples = samples_dev * lax.axis_size("dp")
    cell_norm = math.sqrt(all_samples * N * N * N)
    return (
        field_grad,
        grad_spec / math.sqrt(all_samples * N),
        total_point / cell_norm,
        total_bias / cell_norm,
    )


def solution(mesh):
    return jax.shard_map(
        shards,
        mesh=mesh,
        in_specs=(
            P("dp", None, "gz", None),
            P("dp", None, "gz", None),
            P("gz", None, None, None),
            P(),
            P(),
        ),
        out_specs=(P("dp", None, "gz", None), P("gz", None, None, None), P(), P()),
        check_vma=False,
    )
```

profile of v0, /device:TPU:0, one launch (start us, length us, event | category | flops | bytes accessed | tf_op | source)
XLA Modules:
  0.0 559.2 jit_solution(4819427986787261615)
XLA Ops:
  7.2 0.0 reduce-scatter.3.cloned.1.call-start
  7.3 0.1 sine_select_fusion
  7.4 6.2 %broadcast_multiply_fusion = f32[16,16,96,96]{3,2,1,0:T(8,128)} fusion(f32[16,96]{1,0:T(8,128)S(1)} %sine_select_fusion), kind=kLoop, calls=%fused_computation.12 | loop fusion | flops 2359296 | bytes 9443328 | tf_op jit(solution)/shard_map/mul | solution.py:24
  13.6 12.8 %mul.213 = f32[256,9216]{1,0:T(8,128)} reshape(f32[16,16,96,96]{3,2,1,0:T(8,128)} %broadcast_multiply_fusion) | data formatting | bytes 18874368 | tf_op jit(solution)/shard_map/mul | solution.py:24
  26.4 11.1 %convolution_bitcast_fusion = f32[384,256]{0,1:T(8,128)S(1)} fusion(f32[256,9216]{1,0:T(8,128)} %mul.213, bf16[384,9216]{1,0:T(8,128)(2,1)} %bitcast.98), kind=kOutput, calls=%fused_computation.20 | convolution fusion | flops 10871635968 | bytes 16908288 | tf_op jit(solution)/shard_map/dot_general | solution.py:47
  37.5 0.2 copy.31
  37.7 0.4 fusion.16
  38.1 0.9 copy.32
  39.0 0.0 reduce-scatter.5.cloned.1.call-start
  39.0 12.9 %reshape.211 = f32[256,9216,1]{1,0,2:T(8,128)} reshape(f32[16,16,96,96]{3,2,1,0:T(8,128)} %broadcast_multiply_fusion) | data formatting | bytes 18874368 | tf_op jit(solution)/shard_map/mul | solution.py:24
  51.9 11.7 %fusion.13 = f32[16,24,9216]{2,0,1:T(8,128)} fusion(bf16[16,24,9216]{2,1,0:T(8,128)(2,1)} %bitcast.99, bf16[16,16]{1,0:T(8,128)(2,1)S(1)} %copy-done), kind=kOutput, calls=%fused_computation.18 | convolution fusion | flops 113246208 | bytes 21234176 | tf_op jit(solution)/shard_map/sixz,io->soxz/dot_general | solution.py:71
  63.6 5.0 reduce-scatter.3.cloned.1.call-done
  68.6 1.1 multiply_reduce_fusion.1
  69.8 7.4 %all_gather.6 = f32[16,1,16,256]{3,2,1,0:T(8,128)S(1)} all-gather(f32[4,1,16,256]{3,2,1,0:T(8,128)S(1)} %bitcast.109), channel_id=1, replica_groups=mesh['dp'=32,'gz'=4] {'gz'}, dimensions={0}, use_global_device_ids=true | all-gather | bytes 327680 | tf_op jit(solution)/shard_map/all_gather | solution.py:68
  77.2 12.2 %fusion.24 = f32[16,16,9216]{2,0,1:T(8,128)S(1)} fusion(f32[256,9216,1]{1,0,2:T(8,128)} %reshape.211, f32[16,1,16,256]{3,2,1,0:T(8,128)S(1)} %all_gather.6), kind=kOutput, calls=%fused_computation.32 | convolution fusion | flops 7247757312 | bytes 19136512 | tf_op jit(solution)/shard_map/dot_general | solution.py:53
  89.4 25.9 %convert_reduce_fusion = (f32[16]{0:T(128)S(1)}, bf16[1,16,24,9216]{3,2,1,0:T(8,128)(2,1)}) fusion(f32[16]{0:T(128)S(1)} %copy-done.3, f32[16,24,9216]{2,0,1:T(8,128)} %fusion.13, f32[16,16,9216]{2,0,1:T(8,128)S(1)} %fusion.24, f32[16,96]{1,0:T(8,128)S(1)} %sine_select_fusion, s32[]{:T(128)S(6)} %select_n.65, bf16[1,16,24,9216]{3,2,1,0:T(8,128)(2,1)S(1)} %bitcast.112), kind=kOutput, calls=%fused_computation.11 | convolution fusion | flops 736100352 | bytes 37755012 | tf_op jit(solution)/shard_map/ax,asoz->soxz/dot_general | solution.py:57
  115.4 13.4 %fusion.47 = f32[16,24,256]{2,1,0:T(8,128)S(1)} fusion(f32[256,9216,1]{1,0,2:T(8,128)S(1)} %bitcast.97, bf16[1,16,24,9216]{3,2,1,0:T(8,128)(2,1)} %get-tuple-element.21), kind=kOutput, calls=%fused_computation.62 | convolution fusion | flops 10871635968 | bytes 16908288 | tf_op jit(solution)/shard_map/dot_general | solution.py:47
  128.9 17.8 %fusion.17 = f32[16,16]{0,1:T(8,128)S(1)} fusion(bf16[16,24,9216]{2,1,0:T(8,128)(2,1)S(1)} %bitcast.102, bf16[16,24,9216]{2,1,0:T(8,128)(2,1)} %bitcast.103), kind=kOutput, calls=%fused_computation.25 | convolution fusion | flops 113246208 | bytes 14156800 | tf_op jit(solution)/shard_map/sixz,soxz->io/dot_general | solution.py:89
  146.7 65.4 %all-reduce = (f32[16,16]{0,1:T(8,128)S(1)}, f32[16]{0:T(128)S(1)}) all-reduce(f32[16,16]{0,1:T(8,128)S(1)} %fusion.17, f32[16]{0:T(128)S(1)} %get-tuple-element.20), channel_id=1, replica_groups=mesh['dp'=32,'gz'=4] {'dp','gz'}, use_global_device_ids=true, to_apply=%region_3.4 | all-reduce | flops 272 | bytes 2176 | tf_op jit(solution)/shard_map/psum | solution.py:91
  212.2 0.7 copy.43
  212.8 0.5 broadcast_multiply_fusion.3
  213.4 0.4 fusion.15
  213.8 0.9 copy.37
  214.7 0.0 all-reduce.3.cloned.1.call-start
  214.7 16.0 %fusion.10 = f32[24,9216,16]{1,2,0:T(8,128)} fusion(bf16[16,24,9216]{2,1,0:T(8,128)(2,1)} %bitcast.104, bf16[16,16]{1,0:T(8,128)(2,1)S(1)} %copy-done), kind=kOutput, calls=%fused_computation.15 | convolution fusion | flops 113246208 | bytes 21234176 | tf_op jit(solution)/shard_map/soxz,io->sixz/dot_general | solution.py:87
  230.7 8.1 %reduce-scatter.5.cloned.1.call-done = f32[4,1,16,256]{3,2,1,0:T(8,128)} async-done(((f32[16,1,16,256]{3,2,1,0:T(8,128)}), f32[4,1,16,256]{3,2,1,0:T(8,128)}) %reduce-scatter.5.cloned.1.call-update) | async-done | bytes 65552 | tf_op jit(solution)/shard_map/reduce_scatter | solution.py:77
  238.8 2.1 multiply_bitcast_fusion
  240.9 7.3 %all_gather.7 = f32[16,1,16,256]{3,2,1,0:T(8,128)S(1)} all-gather(f32[4,1,16,256]{3,2,1,0:T(8,128)S(1)} %bitcast.108), channel_id=1, replica_groups=mesh['dp'=32,'gz'=4] {'gz'}, dimensions={0}, use_global_device_ids=true | all-gather | bytes 327680 | tf_op jit(solution)/shard_map/all_gather | solution.py:84
  248.2 12.2 %fusion.22 = f32[16,16,9216]{2,0,1:T(8,128)S(1)} fusion(f32[256,9216,1]{1,0,2:T(8,128)} %reshape.211, f32[16,1,16,256]{3,2,1,0:T(8,128)S(1)} %all_gather.7), kind=kOutput, calls=%fused_computation.30 | convolution fusion | flops 7247757312 | bytes 19136512 | tf_op jit(solution)/shard_map/dot_general | solution.py:53
  260.4 25.8 %fusion.6 = bf16[1,16,24,9216]{3,2,1,0:T(8,128)(2,1)} fusion(f32[24,9216,16]{1,2,0:T(8,128)} %fusion.10, f32[16,16,9216]{2,0,1:T(8,128)S(1)} %fusion.22, f32[16,96]{1,0:T(8,128)S(1)} %sine_select_fusion, s32[]{:T(128)S(6)} %select_n.65), kind=kOutput, calls=%fused_computation.8 | convolution fusion | flops 690094080 | bytes 30676996 | tf_op jit(solution)/shard_map/ax,asoz->soxz/dot_general | solution.py:57
  286.2 263.8 %all-reduce.3.cloned.1.call-done = f32[4,16,16,256]{3,2,1,0:T(8,128)} async-done(((f32[4,16,16,256]{3,2,1,0:T(8,128)}), f32[4,16,16,256]{3,2,1,0:T(8,128)}) %all-reduce.3.cloned.1.call-update) | async-done | bytes 1048592 | tf_op jit(solution)/shard_map/psum | solution.py:93
  550.0 2.3 broadcast_multiply_fusion.1
  (31 shorter events, 0.1 us)
Async XLA Ops:
  7.2 44.8 %copy-start = (bf16[16,16]{1,0:T(8,128)(2,1)S(1)}, bf16[16,16]{1,0:T(8,128)(2,1)}, u32[]{:S(2)}) copy-start(bf16[16,16]{1,0:T(8,128)(2,1)} %param.8) | copy-start | bytes 1540
  7.2 61.4 %reduce-scatter.3.cloned.1.call-start = ((), (), s32[]{:S(2)}) async-start(), calls=%async_computation.2 | async-start | bytes 327680 | tf_op jit(solution)/shard_map/reduce_scatter | solution.py:61
  39.0 199.8 %reduce-scatter.5.cloned.1.call-start = ((), (), s32[]{:S(2)}) async-start(), calls=%async_computation.3 | async-start | bytes 327680 | tf_op jit(solution)/shard_map/reduce_scatter | solution.py:77
  51.9 16.7 %copy-start.1 = (f32[4,16,16,256]{3,2,1,0:T(8,128)S(1)}, f32[4,16,16,256]{3,2,1,0:T(8,128)}, u32[]{:S(2)}) copy-start(f32[4,16,16,256]{3,2,1,0:T(8,128)} %param.7) | copy-start | bytes 3145732
  68.6 20.8 %slice-start.5 = ((s8[7077888]{0:T(1024)(128)(4,1)}), s8[4194304]{0:T(1024)(128)(4,1)S(1)}, s32[]{:S(2)}) async-start(s8[7077888]{0:T(1024)(128)(4,1)} %bitcast.111), calls=%async_computation.10 | async-start | bytes 8388608
  77.2 12.2 %slice-start.6 = ((s8[7077888]{0:T(1024)(128)(4,1)}), s8[2883584]{0:T(1024)(128)(4,1)S(1)}, s32[]{:S(2)}) async-start(s8[7077888]{0:T(1024)(128)(4,1)} %bitcast.111), calls=%async_computation.11 | async-start | bytes 5767168
  77.2 12.2 %copy-start.3 = (f32[16]{0:T(128)S(1)}, f32[16]{0:T(128)}, u32[]{:S(2)}) copy-start(f32[16]{0:T(128)} %param.9) | copy-start | bytes 196
  77.2 38.2 %slice-start = ((s8[9437184]{0:T(1024)(128)(4,1)}), s8[4194304]{0:T(1024)(128)(4,1)S(1)}, s32[]{:S(2)}) async-start(s8[9437184]{0:T(1024)(128)(4,1)} %bitcast.96), calls=%async_computation.5 | async-start | bytes 8388608
  89.4 26.0 %slice-start.1 = ((s8[9437184]{0:T(1024)(128)(4,1)}), s8[4194304]{0:T(1024)(128)(4,1)S(1)}, s32[]{:S(2)}) async-start(s8[9437184]{0:T(1024)(128)(4,1)} %bitcast.96), calls=%async_computation.6 | async-start | bytes 8388608
  89.4 26.0 %slice-start.2 = ((s8[9437184]{0:T(1024)(128)(4,1)}), s8[1048576]{0:T(1024)(128)(4,1)S(1)}, s32[]{:S(2)}) async-start(s8[9437184]{0:T(1024)(128)(4,1)} %bitcast.96), calls=%async_computation.7 | async-start | bytes 2097152
  115.4 13.5 %slice-start.3 = ((s8[7077888]{0:T(1024)(128)(4,1)}), s8[4194304]{0:T(1024)(128)(4,1)S(1)}, s32[]{:S(2)}) async-start(s8[7077888]{0:T(1024)(128)(4,1)} %bitcast.100), calls=%async_computation.8 | async-start | bytes 8388608
  115.4 13.4 %slice-start.4 = ((s8[7077888]{0:T(1024)(128)(4,1)}), s8[2883584]{0:T(1024)(128)(4,1)S(1)}, s32[]{:S(2)}) async-start(s8[7077888]{0:T(1024)(128)(4,1)} %bitcast.100), calls=%async_computation.9 | async-start | bytes 5767168
  214.7 24.1 %copy-start.2 = (f32[4,1,16,256]{3,2,1,0:T(8,128)S(1)}, f32[4,1,16,256]{3,2,1,0:T(8,128)}, u32[]{:S(2)}) copy-start(f32[4,1,16,256]{3,2,1,0:T(8,128)} %reduce-scatter.3.cloned.1.call-done) | copy-start | bytes 196612
  214.7 335.3 %all-reduce.3.cloned.1.call-start = ((), (), s32[]{:S(2)}) async-start(), calls=%async_computation.4 | async-start | bytes 2097152 | tf_op jit(solution)/shard_map/psum | solution.py:93
Sparse Core Ops, SparseCore 0:
  39.1 29.4 reduce-scatter.2
  214.8 23.9 reduce-scatter.4
  241.8 308.1 all-reduce.2
where the time goes:
time: 568 us; the launch traced here: 559 us
  waiting for transfers between devices  277 us (49%)
  matrix products  147 us (26%)
  blocking collectives  80.2 us (14%)
  local copies, waits for them, and re-layouts  28.3 us (5%)
  between operations  14.3 us (3%)
  other arithmetic  12.4 us (2%)
    psum x1, waiting for transfers between devices, shards(): grad_spec = lax.psum(local_spec, 'dp')  264 us
    psum x1, blocking collectives, shards(): total_point, total_bias = lax.psum((local_point, local_bias), ('dp', 'gz'))  65.4 us
    dot_general x2, matrix products, add_inverse(): return jnp.einsum('ax,asoz->soxz', row_basis, inner, precision=highest)  51.8 us
    mul x2, local copies, waits for them, and re-layouts, kron_table(): outer = basis[:, None, :, None] * basis[None, :, None, :]  25.7 us
    dot_general x2, matrix products, to_modes(): lax.dot_general(flattened, kron, contract_cells, precision=highest)  24.5 us
    dot_general x2, matrix products, add_inverse(): jnp.dot(piece.reshape(piece_rows * samples_dev * channels, M * M), kron,...  24.4 us
    dot_general x1, matrix products, shards(): jnp.einsum('sixz,soxz->io', field, grad_pre, preferred_element_type=jnp.f...  17.8 us
    dot_general x1, matrix products, shards(): jnp.einsum('soxz,io->sixz', grad_pre, point_weight, preferred_element_typ...  16 us
  transfers between devices with their start and end apart: 3, of which 3 were waited for; matrix products, arithmetic and copies ran while one was open for 14% of the time, Pallas kernels for 0%

commit v1 on v0

--- a/solution.py
+++ b/solution.py
@@ -88,7 +88,13 @@
     ).astype(jnp.bfloat16)
     local_point = jnp.einsum("sixz,soxz->io", field, grad_pre, preferred_element_type=jnp.float32)
     local_bias = jnp.sum(grad_pre, axis=(0, 2, 3), dtype=jnp.float32)
-    total_point, total_bias = lax.psum((local_point, local_bias), ("dp", "gz"))
+
+    def review_wall(mat, device_axis, peer_axis):
+        for at in (device_axis, peer_axis):
+            mat = lax.psum(mat, at)
+        return mat
+
+    total_point, total_bias = review_wall((local_point, local_bias), "dp", "gz")
     local_spec = jnp.einsum("asip,asop->aiop", coefficients, grad_modes, precision=highest)
     grad_spec = lax.psum(local_spec, "dp")
     all_samples = samples_dev * lax.axis_size("dp")

time: 568 us -> 592 us (1.042)
  blocking collectives: 80.2 us -> 106 us
    psum x1 -> x2, blocking collectives: 65.4 us -> 91.3 us  [review_wall(): mat = lax.psum(mat, at)]
  transfers between devices with their start and end apart: 3 -> 3, of which waited for: 3 -> 3; matrix products, arithmetic and copies ran while one was open for 14% -> 13% of each run, Pallas kernels for 0% -> 0%
where the time goes in v1:
time: 592 us; the launch traced here: 583 us
  waiting for transfers between devices  275 us (46%)
  matrix products  147 us (25%)
  blocking collectives  106 us (18%)
  local copies, waits for them, and re-layouts  28.3 us (5%)
  between operations  14.4 us (2%)
  other arithmetic  12.4 us (2%)
    psum x1, waiting for transfers between devices, shards(): grad_spec = lax.psum(local_spec, 'dp')  264 us
    psum x2, blocking collectives, review_wall(): mat = lax.psum(mat, at)  91.3 us
    dot_general x2, matrix products, add_inverse(): return jnp.einsum('ax,asoz->soxz', row_basis, inner, precision=highest)  51.8 us
    mul x2, local copies, waits for them, and re-layouts, kron_table(): outer = basis[:, None, :, None] * basis[None, :, None, :]  25.7 us
    dot_general x2, matrix products, to_modes(): lax.dot_general(flattened, kron, contract_cells, precision=highest)  24.5 us
    dot_general x2, matrix products, add_inverse(): jnp.dot(piece.reshape(piece_rows * samples_dev * channels, M * M), kron,...  24.4 us
    dot_general x1, matrix products, shards(): jnp.einsum('sixz,soxz->io', field, grad_pre, preferred_element_type=jnp.f...  17.8 us
    dot_general x1, matrix products, shards(): jnp.einsum('soxz,io->sixz', grad_pre, point_weight, preferred_element_typ...  16 us
  transfers between devices with their start and end apart: 3, of which 3 were waited for; matrix products, arithmetic and copies ran while one was open for 13% of the time, Pallas kernels for 0%

profile of v1, /device:TPU:0, one launch (start us, length us, event | category | flops | bytes accessed | tf_op | source)
XLA Modules:
  0.0 583.4 jit_solution(17319083025714063063)
XLA Ops:
  7.3 0.1 sine_select_fusion
  7.4 6.2 %broadcast_multiply_fusion = f32[16,16,96,96]{3,2,1,0:T(8,128)} fusion(f32[16,96]{1,0:T(8,128)S(1)} %sine_select_fusion), kind=kLoop, calls=%fused_computation.12 | loop fusion | flops 2359296 | bytes 9443328 | tf_op jit(solution)/shard_map/mul | solution.py:24
  13.6 12.8 %mul.213 = f32[256,9216]{1,0:T(8,128)} reshape(f32[16,16,96,96]{3,2,1,0:T(8,128)} %broadcast_multiply_fusion) | data formatting | bytes 18874368 | tf_op jit(solution)/shard_map/mul | solution.py:24
  26.4 11.1 %convolution_bitcast_fusion = f32[384,256]{0,1:T(8,128)S(1)} fusion(f32[256,9216]{1,0:T(8,128)} %mul.213, bf16[384,9216]{1,0:T(8,128)(2,1)} %bitcast.98), kind=kOutput, calls=%fused_computation.20 | convolution fusion | flops 10871635968 | bytes 16908288 | tf_op jit(solution)/shard_map/dot_general | solution.py:47
  37.5 0.2 copy.31
  37.7 0.4 fusion.16
  38.1 0.9 copy.32
  39.0 0.0 reduce-scatter.5.cloned.1.call-start
  39.1 12.9 %reshape.211 = f32[256,9216,1]{1,0,2:T(8,128)} reshape(f32[16,16,96,96]{3,2,1,0:T(8,128)} %broadcast_multiply_fusion) | data formatting | bytes 18874368 | tf_op jit(solution)/shard_map/mul | solution.py:24
  52.0 11.8 %fusion.13 = f32[16,24,9216]{2,0,1:T(8,128)} fusion(bf16[16,24,9216]{2,1,0:T(8,128)(2,1)} %bitcast.99, bf16[16,16]{1,0:T(8,128)(2,1)S(1)} %copy-done), kind=kOutput, calls=%fused_computation.18 | convolution fusion | flops 113246208 | bytes 21234176 | tf_op jit(solution)/shard_map/sixz,io->soxz/dot_general | solution.py:71
  63.7 4.9 reduce-scatter.3.cloned.1.call-done
  68.6 1.1 multiply_reduce_fusion.1
  69.8 7.4 %all_gather.6 = f32[16,1,16,256]{3,2,1,0:T(8,128)S(1)} all-gather(f32[4,1,16,256]{3,2,1,0:T(8,128)S(1)} %bitcast.109), channel_id=1, replica_groups=mesh['dp'=32,'gz'=4] {'gz'}, dimensions={0}, use_global_device_ids=true | all-gather | bytes 327680 | tf_op jit(solution)/shard_map/all_gather | solution.py:68
  77.2 12.2 %fusion.24 = f32[16,16,9216]{2,0,1:T(8,128)S(1)} fusion(f32[256,9216,1]{1,0,2:T(8,128)} %reshape.211, f32[16,1,16,256]{3,2,1,0:T(8,128)S(1)} %all_gather.6), kind=kOutput, calls=%fused_computation.32 | convolution fusion | flops 7247757312 | bytes 19136512 | tf_op jit(solution)/shard_map/dot_general | solution.py:53
  89.5 25.9 %convert_reduce_fusion = (f32[16]{0:T(128)S(1)}, bf16[1,16,24,9216]{3,2,1,0:T(8,128)(2,1)}) fusion(f32[16]{0:T(128)S(1)} %copy-done.3, f32[16,24,9216]{2,0,1:T(8,128)} %fusion.13, f32[16,16,9216]{2,0,1:T(8,128)S(1)} %fusion.24, f32[16,96]{1,0:T(8,128)S(1)} %sine_select_fusion, s32[]{:T(128)S(6)} %select_n.65, bf16[1,16,24,9216]{3,2,1,0:T(8,128)(2,1)S(1)} %bitcast.112), kind=kOutput, calls=%fused_computation.11 | convolution fusion | flops 736100352 | bytes 37755012 | tf_op jit(solution)/shard_map/ax,asoz->soxz/dot_general | solution.py:57
  115.4 13.4 %fusion.47 = f32[16,24,256]{2,1,0:T(8,128)S(1)} fusion(f32[256,9216,1]{1,0,2:T(8,128)S(1)} %bitcast.97, bf16[1,16,24,9216]{3,2,1,0:T(8,128)(2,1)} %get-tuple-element.23), kind=kOutput, calls=%fused_computation.62 | convolution fusion | flops 10871635968 | bytes 16908288 | tf_op jit(solution)/shard_map/dot_general | solution.py:47
  128.9 17.8 %fusion.17 = f32[16,16]{0,1:T(8,128)S(1)} fusion(bf16[16,24,9216]{2,1,0:T(8,128)(2,1)S(1)} %bitcast.102, bf16[16,24,9216]{2,1,0:T(8,128)(2,1)} %bitcast.103), kind=kOutput, calls=%fused_computation.25 | convolution fusion | flops 113246208 | bytes 14156800 | tf_op jit(solution)/shard_map/sixz,soxz->io/dot_general | solution.py:89
  146.7 83.9 %all-reduce = (f32[16,16]{0,1:T(8,128)S(1)}, f32[16]{0:T(128)S(1)}) all-reduce(f32[16,16]{0,1:T(8,128)S(1)} %fusion.17, f32[16]{0:T(128)S(1)} %get-tuple-element.22), channel_id=1, replica_groups=mesh['dp'=32,'gz'=4] {'dp'}, use_global_device_ids=true, to_apply=%region_3.4 | all-reduce | flops 272 | bytes 2176 | tf_op jit(solution)/shard_map/psum | solution.py:94
  230.6 7.4 %all-reduce.1 = (f32[16,16]{0,1:T(8,128)S(1)}, f32[16]{0:T(128)S(1)}) all-reduce(f32[16,16]{0,1:T(8,128)S(1)} %get-tuple-element.16, f32[16]{0:T(128)S(1)} %get-tuple-element.17), channel_id=1, replica_groups=mesh['dp'=32,'gz'=4] {'gz'}, use_global_device_ids=true, to_apply=%region_4.5 | all-reduce | flops 272 | bytes 2176 | tf_op jit(solution)/shard_map/psum | solution.py:94
  238.0 0.7 copy.43
  238.7 0.5 broadcast_multiply_fusion.3
  239.2 0.4 fusion.15
  239.6 0.9 copy.37
  240.5 0.0 all-reduce.4.cloned.1.call-start
  240.6 16.0 %fusion.10 = f32[24,9216,16]{1,2,0:T(8,128)} fusion(bf16[16,24,9216]{2,1,0:T(8,128)(2,1)} %bitcast.104, bf16[16,16]{1,0:T(8,128)(2,1)S(1)} %copy-done), kind=kOutput, calls=%fused_computation.15 | convolution fusion | flops 113246208 | bytes 21234176 | tf_op jit(solution)/shard_map/soxz,io->sixz/dot_general | solution.py:87
  256.6 6.4 %reduce-scatter.5.cloned.1.call-done = f32[4,1,16,256]{3,2,1,0:T(8,128)} async-done(((f32[16,1,16,256]{3,2,1,0:T(8,128)}), f32[4,1,16,256]{3,2,1,0:T(8,128)}) %reduce-scatter.5.cloned.1.call-update) | async-done | bytes 65552 | tf_op jit(solution)/shard_map/reduce_scatter | solution.py:77
  263.0 2.1 multiply_bitcast_fusion
  265.1 7.3 %all_gather.7 = f32[16,1,16,256]{3,2,1,0:T(8,128)S(1)} all-gather(f32[4,1,16,256]{3,2,1,0:T(8,128)S(1)} %bitcast.108), channel_id=1, replica_groups=mesh['dp'=32,'gz'=4] {'gz'}, dimensions={0}, use_global_device_ids=true | all-gather | bytes 327680 | tf_op jit(solution)/shard_map/all_gather | solution.py:84
  272.4 12.2 %fusion.22 = f32[16,16,9216]{2,0,1:T(8,128)S(1)} fusion(f32[256,9216,1]{1,0,2:T(8,128)} %reshape.211, f32[16,1,16,256]{3,2,1,0:T(8,128)S(1)} %all_gather.7), kind=kOutput, calls=%fused_computation.30 | convolution fusion | flops 7247757312 | bytes 19136512 | tf_op jit(solution)/shard_map/dot_general | solution.py:53
  284.6 25.8 %fusion.6 = bf16[1,16,24,9216]{3,2,1,0:T(8,128)(2,1)} fusion(f32[24,9216,16]{1,2,0:T(8,128)} %fusion.10, f32[16,16,9216]{2,0,1:T(8,128)S(1)} %fusion.22, f32[16,96]{1,0:T(8,128)S(1)} %sine_select_fusion, s32[]{:T(128)S(6)} %select_n.65), kind=kOutput, calls=%fused_computation.8 | convolution fusion | flops 690094080 | bytes 30676996 | tf_op jit(solution)/shard_map/ax,asoz->soxz/dot_general | solution.py:57
  310.4 263.7 %all-reduce.4.cloned.1.call-done = f32[4,16,16,256]{3,2,1,0:T(8,128)} async-done(((f32[4,16,16,256]{3,2,1,0:T(8,128)}), f32[4,16,16,256]{3,2,1,0:T(8,128)}) %all-reduce.4.cloned.1.call-update) | async-done | bytes 1048592 | tf_op jit(solution)/shard_map/psum | solution.py:99
  574.1 2.3 broadcast_multiply_fusion.1
  (32 shorter events, 0.2 us)
Async XLA Ops:
  7.2 44.8 %copy-start = (bf16[16,16]{1,0:T(8,128)(2,1)S(1)}, bf16[16,16]{1,0:T(8,128)(2,1)}, u32[]{:S(2)}) copy-start(bf16[16,16]{1,0:T(8,128)(2,1)} %param.8) | copy-start | bytes 1540
  7.2 61.4 %reduce-scatter.3.cloned.1.call-start = ((), (), s32[]{:S(2)}) async-start(), calls=%async_computation.2 | async-start | bytes 327680 | tf_op jit(solution)/shard_map/reduce_scatter | solution.py:61
  39.0 224.0 %reduce-scatter.5.cloned.1.call-start = ((), (), s32[]{:S(2)}) async-start(), calls=%async_computation.3 | async-start | bytes 327680 | tf_op jit(solution)/shard_map/reduce_scatter | solution.py:77
  52.0 16.7 %copy-start.1 = (f32[4,16,16,256]{3,2,1,0:T(8,128)S(1)}, f32[4,16,16,256]{3,2,1,0:T(8,128)}, u32[]{:S(2)}) copy-start(f32[4,16,16,256]{3,2,1,0:T(8,128)} %param.7) | copy-start | bytes 3145732
  68.6 20.8 %slice-start.5 = ((s8[7077888]{0:T(1024)(128)(4,1)}), s8[4194304]{0:T(1024)(128)(4,1)S(1)}, s32[]{:S(2)}) async-start(s8[7077888]{0:T(1024)(128)(4,1)} %bitcast.111), calls=%async_computation.10 | async-start | bytes 8388608
  77.2 12.2 %slice-start.6 = ((s8[7077888]{0:T(1024)(128)(4,1)}), s8[2883584]{0:T(1024)(128)(4,1)S(1)}, s32[]{:S(2)}) async-start(s8[7077888]{0:T(1024)(128)(4,1)} %bitcast.111), calls=%async_computation.11 | async-start | bytes 5767168
  77.2 12.2 %copy-start.3 = (f32[16]{0:T(128)S(1)}, f32[16]{0:T(128)}, u32[]{:S(2)}) copy-start(f32[16]{0:T(128)} %param.9) | copy-start | bytes 196
  77.2 38.2 %slice-start = ((s8[9437184]{0:T(1024)(128)(4,1)}), s8[4194304]{0:T(1024)(128)(4,1)S(1)}, s32[]{:S(2)}) async-start(s8[9437184]{0:T(1024)(128)(4,1)} %bitcast.96), calls=%async_computation.5 | async-start | bytes 8388608
  89.4 26.0 %slice-start.1 = ((s8[9437184]{0:T(1024)(128)(4,1)}), s8[4194304]{0:T(1024)(128)(4,1)S(1)}, s32[]{:S(2)}) async-start(s8[9437184]{0:T(1024)(128)(4,1)} %bitcast.96), calls=%async_computation.6 | async-start | bytes 8388608
  89.4 26.0 %slice-start.2 = ((s8[9437184]{0:T(1024)(128)(4,1)}), s8[1048576]{0:T(1024)(128)(4,1)S(1)}, s32[]{:S(2)}) async-start(s8[9437184]{0:T(1024)(128)(4,1)} %bitcast.96), calls=%async_computation.7 | async-start | bytes 2097152
  115.4 13.5 %slice-start.3 = ((s8[7077888]{0:T(1024)(128)(4,1)}), s8[4194304]{0:T(1024)(128)(4,1)S(1)}, s32[]{:S(2)}) async-start(s8[7077888]{0:T(1024)(128)(4,1)} %bitcast.100), calls=%async_computation.8 | async-start | bytes 8388608
  115.4 13.4 %slice-start.4 = ((s8[7077888]{0:T(1024)(128)(4,1)}), s8[2883584]{0:T(1024)(128)(4,1)S(1)}, s32[]{:S(2)}) async-start(s8[7077888]{0:T(1024)(128)(4,1)} %bitcast.100), calls=%async_computation.9 | async-start | bytes 5767168
  240.5 22.5 %copy-start.2 = (f32[4,1,16,256]{3,2,1,0:T(8,128)S(1)}, f32[4,1,16,256]{3,2,1,0:T(8,128)}, u32[]{:S(2)}) copy-start(f32[4,1,16,256]{3,2,1,0:T(8,128)} %reduce-scatter.3.cloned.1.call-done) | copy-start | bytes 196612
  240.5 333.6 %all-reduce.4.cloned.1.call-start = ((), (), s32[]{:S(2)}) async-start(), calls=%async_computation.4 | async-start | bytes 2097152 | tf_op jit(solution)/shard_map/psum | solution.py:99
Sparse Core Ops, SparseCore 0:
  39.1 29.4 reduce-scatter.2
  240.6 22.2 reduce-scatter.4
  266.0 308.0 all-reduce.3
